TPU v7x, 256 devices: a whole 4x4x8 slice. The times are simulated.
256 devices in a mesh: group: 32 (over z, x_lo, core), rep: 8 (over x_hi, y).
Axes of the slice: x: 4 (x_hi: 2, x_lo: 2; x = x_hi * 2 + x_lo), y: 4, z: 8, core: 2. Of those that a mesh axis runs over, the one named last changes fastest.
Arguments:
- queries: bfloat16 [256, 256, 3072], P(('group', 'rep')), may hold values from -46 to 46
- keys: bfloat16 [256, 256, 3072], P(('group', 'rep')), may hold values from -46 to 46
- values: bfloat16 [256, 256, 3072], P(('group', 'rep')), may hold values from -24 to 24
- grad_output: bfloat16 [256, 256, 3072], P(('group', 'rep')), may hold values from -6 to 6
- weight_codes: bfloat16 [3072, 3072], P('group'), may hold values from -4 to 4
- weight_scales: float32 [3072, 12], P('group'), may hold values from 0.006 to 0.06
Outputs:
- grad_queries: bfloat16 [256, 256, 3072], P(('group', 'rep'))
- grad_keys: bfloat16 [256, 256, 3072], P(('group', 'rep'))
- grad_values: bfloat16 [256, 256, 3072], P(('group', 'rep'))
- grad_weight: float32 [3072, 3072], P(('group', 'rep'))
All inputs are finite; a program needn't handle non-finite values.
Results may differ from a plain program's by a relative error of at most 0.029.
Values may be sent and summed in bfloat16 or wider, within the bound.
No kernel may reach another device: no remote copies, remote signals or barrier semaphores. Data moves between devices by JAX's collectives and lax.ppermute only.
A program may use at most 128 MiB of HBM per device.

v0:
```python
import jax
import jax.numpy as jnp
from jax import lax
from jax.sharding import Mesh
from jax.sharding import PartitionSpec as P

HD = 128
GROUP = ("group_0", "group_1", "group_2")
GROUP_REP = ("group_0", "group_1", "group_2", "rep")


def from_everyone(value, axis):
    count = lax.axis_size(axis)
    return lax.all_to_all(
        jnp.broadcast_to(value[None], (count, *value.shape)), axis, 0, 0, tiled=True
    )


def in_order(pieces, dim):
    shape = list(pieces.shape[1:])
    shape[dim] *= pieces.shape[0]
    return jnp.moveaxis(pieces, 0, dim).reshape(shape)


def gather_axes(value, axes, dim):
    far, near = axes
    pieces = from_everyone(from_everyone(value, far), near)
    return in_order(pieces.swapaxes(0, 1).reshape(-1, *value.shape), dim)


def cut_along(value, dim, count):
    before, after = (value.shape[:dim], value.shape[dim + 1 :])
    return jnp.moveaxis(value.reshape(*before, count, -1, *after), dim, 0)


def sent_and_summed(value, axis, dim):
    count = lax.axis_size(axis)
    pieces = lax.all_to_all(cut_along(value, dim, count), axis, 0, 0, tiled=True)
    return jnp.sum(pieces, axis=0)


def sum_in_two_steps(value, axes, dim):
    far, near = axes
    pieces = cut_along(value, dim, lax.axis_size(far))
    nearer = sent_and_summed(pieces, near, dim + 1)
    arrived = lax.all_to_all(nearer, far, split_axis=0, concat_axis=0, tiled=True)
    return arrived.sum(axis=0)


def restore(code_rows, scale_rows):
    row_count = code_rows.shape[0]
    block_count = scale_rows.shape[1]
    spread = (
        code_rows.astype(jnp.float32).reshape(row_count, block_count, -1) * scale_rows[:, :, None]
    )
    return spread.reshape(row_count, -1).astype(jnp.bfloat16)


def forward_image(arrays_in):
    query, keyset, valueset = arrays_in
    seq_len = query.shape[0]
    head_count = query.shape[1] // HD
    query_heads = query.reshape(seq_len, head_count, HD)
    key_heads = keyset.reshape(seq_len, head_count, HD)
    value_heads = valueset.reshape(seq_len, head_count, HD)
    scores = jnp.einsum(
        "qhd,khd->hqk", query_heads, key_heads, preferred_element_type=jnp.float32
    ) * HD ** (-0.5)
    highest = jnp.max(scores, axis=2, keepdims=True)
    exponent = jnp.exp(scores - highest)
    probability = exponent / jnp.sum(exponent, axis=2, keepdims=True)
    weight_half = probability.astype(jnp.bfloat16)
    context = jnp.einsum(
        "hqk,khd->qhd", weight_half, value_heads, preferred_element_type=jnp.float32
    )
    return (probability, context.astype(jnp.bfloat16).reshape(seq_len, -1))


def backward_image(arrays_in):
    query, keyset, valueset, probability, grad_context = arrays_in
    seq_len = query.shape[0]
    head_count = query.shape[1] // HD
    query_heads = query.reshape(seq_len, head_count, HD)
    key_heads = keyset.reshape(seq_len, head_count, HD)
    value_heads = valueset.reshape(seq_len, head_count, HD)
    grad_heads = grad_context.reshape(seq_len, head_count, HD)
    weight_half = probability.astype(jnp.bfloat16)
    grad_value = jnp.einsum(
        "hqk,qhd->khd", weight_half, grad_heads, preferred_element_type=jnp.float32
    )
    dprobs = jnp.einsum("qhd,khd->hqk", grad_heads, value_heads, preferred_element_type=jnp.float32)
    row_delta = jnp.sum(probability * dprobs, axis=2, keepdims=True)
    dscores = (probability * (dprobs - row_delta) * HD ** (-0.5)).astype(jnp.bfloat16)
    grad_query = jnp.einsum("hqk,khd->qhd", dscores, key_heads, preferred_element_type=jnp.float32)
    grad_key = jnp.einsum("hqk,qhd->khd", dscores, query_heads, preferred_element_type=jnp.float32)
    return (
        grad_query.astype(jnp.bfloat16).reshape(seq_len, -1),
        grad_key.astype(jnp.bfloat16).reshape(seq_len, -1),
        grad_value.astype(jnp.bfloat16).reshape(seq_len, -1),
    )


def per_device(queries, keys, values, grad_output, weight_codes, weight_scales):
    image_count, seq_len, row_total = queries.shape
    feature_count = grad_output.shape[2]
    local_rows = image_count * seq_len
    probability, contexts = lax.map(forward_image, (queries, keys, values))
    context_flat = contexts.reshape(local_rows, row_total)
    output_flat = grad_output.reshape(local_rows, feature_count)
    group_count = lax.axis_size(GROUP)
    replica_count = lax.axis_size("rep")
    slab_rows = row_total // (group_count * replica_count)
    first_row = lax.axis_index("rep") * slab_rows
    codes_part = lax.dynamic_slice_in_dim(weight_codes, first_row, slab_rows, 0)
    scales_part = lax.dynamic_slice_in_dim(weight_scales, first_row, slab_rows, 0)
    all_output = lax.all_gather(output_flat, "rep", axis=0, tiled=True)
    split_context = jnp.moveaxis(
        context_flat.reshape(local_rows, group_count, replica_count, slab_rows), 2, 0
    )
    split_context = split_context.reshape(replica_count, local_rows, group_count * slab_rows)
    gathered_ctx = lax.all_to_all(split_context, "rep", split_axis=0, concat_axis=1, tiled=True)
    gathered_ctx = gathered_ctx.reshape(replica_count, local_rows, group_count * slab_rows)
    grad_columns = jnp.dot(
        all_output,
        restore(
            gather_axes(codes_part, (("group_0", "group_1"), "group_2"), 0),
            gather_axes(
                scales_part.astype(jnp.bfloat16), (("group_0", "group_1"), "group_2"), 0
            ).astype(scales_part.dtype),
        ).T,
        preferred_element_type=jnp.float32,
    ).astype(jnp.bfloat16)
    output_blocks = all_output.reshape(replica_count, local_rows, feature_count)
    device_terms = jnp.einsum(
        "rlp,rle->rpe", gathered_ctx, output_blocks, preferred_element_type=jnp.float32
    ).astype(jnp.bfloat16)
    grad_weight = sum_in_two_steps(
        jnp.sum(lax.optimization_barrier(device_terms).astype(jnp.float32), axis=0),
        (("group_0", "group_1"), "group_2"),
        0,
    )
    returned = lax.all_to_all(
        grad_columns.reshape(1, replica_count * local_rows, group_count * slab_rows),
        "rep",
        split_axis=1,
        concat_axis=0,
        tiled=True,
    )
    returned = jnp.moveaxis(
        returned.reshape(replica_count, local_rows, group_count, slab_rows), 0, 2
    )
    grad_context = returned.reshape(image_count, seq_len, row_total)
    grad_queries, grad_keys, grad_values = lax.map(
        backward_image, (queries, keys, values, probability, grad_context)
    )
    return (grad_queries, grad_keys, grad_values, grad_weight)


def solution(mesh):
    split = Mesh(
        mesh.devices.reshape(8, 2, 2, mesh.shape["rep"]), ("group_0", "group_1", "group_2", "rep")
    )
    return jax.shard_map(
        per_device,
        mesh=split,
        in_specs=(
            P(GROUP_REP, None, None),
            P(GROUP_REP, None, None),
            P(GROUP_REP, None, None),
            P(GROUP_REP, None, None),
            P(GROUP, None),
            P(GROUP, None),
        ),
        out_specs=(
            P(GROUP_REP, None, None),
            P(GROUP_REP, None, None),
            P(GROUP_REP, None, None),
            P(GROUP_REP, None),
        ),
        check_vma=False,
    )
```

profile of v0, /device:TPU:4, one launch (start us, length us, event | category | flops | bytes accessed | tf_op | source)
XLA Modules:
  0.0 398.7 jit_solution(12941961424991909647)
XLA Ops:
  7.9 0.9 dynamic-slice_convert_fusion
  9.5 9.2 %all-to-all-start.2 = ((bf16[16,12,12]{1,2,0:T(8,128)(2,1)}), bf16[16,12,12]{1,2,0:T(8,128)(2,1)S(1)}, u32[]{:S(2)}, u32[]{:S(2)}) async-start(bf16[16,12,12]{1,2,0:T(8,128)(2,1)} %broadcast_in_dim.52), calls=%async_computation.2 | async-start | bytes 131072 | tf_op jit(solution)/shard_map/all_to_all | solution.py:14
  18.7 9.0 %all-to-all-done.2 = bf16[16,12,12]{1,2,0:T(8,128)(2,1)S(1)} async-done(((bf16[16,12,12]{1,2,0:T(8,128)(2,1)}), bf16[16,12,12]{1,2,0:T(8,128)(2,1)S(1)}, u32[]{:S(2)}, u32[]{:S(2)}) %all-to-all-start.2) | async-done | bytes 4640 | tf_op jit(solution)/shard_map/all_to_all | solution.py:14
  27.9 3.7 all_to_all.48
  31.6 1.3 broadcast_in_dim.50
  33.0 4.4 %all-to-all-start = ((bf16[16,12,3072]{2,1,0:T(8,128)(2,1)}), bf16[16,12,3072]{2,1,0:T(8,128)(2,1)}, u32[]{:S(2)}, u32[]{:S(2)}) async-start(bf16[16,12,3072]{2,1,0:T(8,128)(2,1)} %broadcast_in_dim.50), calls=%async_computation | async-start | bytes 3145728 | tf_op jit(solution)/shard_map/all_to_all | solution.py:14
  37.4 1.6 copy.148
  39.0 2.6 copy.147
  41.6 1.7 copy.149
  43.3 7.4 %fusion.43 = (f32[24,256]{1,0:T(8,128)S(1)}, f32[24,256,256]{1,2,0:T(8,128)}) fusion(bf16[256,24,128]{0,2,1:T(8,128)(2,1)} %bitcast.77, bf16[256,24,128]{0,2,1:T(8,128)(2,1)} %bitcast.79), kind=kOutput, calls=%fused_computation.38 | convolution fusion | flops 407372032 | bytes 9461760 | tf_op jit(solution)/shard_map/while/body/eval_jaxpr/sub | solution.py:70
  50.7 4.6 %fusion.33 = bf16[256,24,128]{0,2,1:T(8,128)(2,1)} fusion(bf16[256,24,128]{0,2,1:T(8,128)(2,1)S(1)} %bitcast.72, f32[24,256,256]{1,2,0:T(8,128)} %get-tuple-element.74, f32[24,256]{1,0:T(8,128)S(1)} %get-tuple-element.73), kind=kOutput, calls=%fused_computation.28 | convolution fusion | flops 406585344 | bytes 9461760 | tf_op jit(solution)/shard_map/while/body/eval_jaxpr/hqk,khd->qhd/dot_general | solution.py:73
  55.3 2.4 reshape_reshape.8
  58.4 1.5 copy.136
  60.5 2.4 mul.32
  63.0 6.1 %copy.122 = f32[384,3072]{1,0:T(8,128)} copy(f32[384,3072]{0,1:T(8,128)} %bitcast.67) | data formatting | bytes 9437184 | tf_op jit(solution)/shard_map/mul | solution.py:54
  69.0 8.3 %all-to-all-done = bf16[16,12,3072]{2,1,0:T(8,128)(2,1)} async-done(((bf16[16,12,3072]{2,1,0:T(8,128)(2,1)}), bf16[16,12,3072]{2,1,0:T(8,128)(2,1)}, u32[]{:S(2)}, u32[]{:S(2)}) %all-to-all-start) | async-done | bytes 1179680 | tf_op jit(solution)/shard_map/all_to_all | solution.py:14
  77.3 2.1 copy.118
  79.7 5.6 %all_to_all.49 = bf16[2,16,12,3072]{3,1,2,0:T(8,128)(2,1)S(1)} all-to-all(bf16[2,16,12,3072]{3,1,2,0:T(8,128)(2,1)S(1)} %broadcast_in_dim.51), channel_id=1, replica_groups=mesh['group_0'=8,'group_1'=2,'group_2'=2,'rep'=8] {'group_2'}, dimensions={0} | all-to-all | bytes 4718592 | tf_op jit(solution)/shard_map/all_to_all | solution.py:14
  85.3 8.0 %all-to-all-start.5 = ((bf16[8,256,384]{1,2,0:T(8,128)(2,1)}), bf16[8,256,384]{1,2,0:T(8,128)(2,1)}, u32[]{:S(2)}, u32[]{:S(2)}) async-start(bf16[8,256,384]{1,2,0:T(8,128)(2,1)} %copy.136), calls=%async_computation.5 | async-start | bytes 3145728 | tf_op jit(solution)/shard_map/all_to_all | solution.py:121
  93.8 5.5 %copy.119 = f32[16,2,12,3072]{3,2,1,0:T(8,128)} copy(f32[16,2,12,3072]{3,0,2,1:T(8,128)S(1)} %convert_bitcast_fusion) | data formatting | bytes 9437184 | tf_op jit(solution)/shard_map/convert_element_type | solution.py:54
  99.3 5.4 %reshape.105 = f32[384,3072]{1,0:T(8,128)} reshape(f32[16,2,12,3072]{3,2,1,0:T(8,128)} %copy.119) | data formatting | bytes 9437184 | tf_op jit(solution)/shard_map/convert_element_type | solution.py:54
  104.8 77.1 %all-gather.3.cloned.1.call-done = bf16[1,2048,3072]{2,1,0:T(8,128)(2,1)} async-done(((bf16[1,256,3072]{2,1,0:T(8,128)(2,1)}), bf16[1,2048,3072]{2,1,0:T(8,128)(2,1)}) %all-gather.3.cloned.1.call-update) | async-done | bytes 12582928 | tf_op jit(solution)/shard_map/all_gather | solution.py:116
  181.9 10.8 %fusion.22 = bf16[1,2048,384]{1,2,0:T(8,128)(2,1)S(1)} fusion(bf16[1,2048,3072]{2,1,0:T(8,128)(2,1)} %all-gather.3.cloned.1.call-done, f32[384,3072]{1,0:T(8,128)} %reshape.105, f32[384,3072]{1,0:T(8,128)} %copy.122), kind=kOutput, calls=%fused_computation.21 | convolution fusion | flops 4834983936 | bytes 23592960 | tf_op jit(solution)/shard_map/dot_general | solution.py:123
  192.7 5.6 %copy.123 = bf16[1,2048,384]{2,0,1:T(2,128)(2,1)} copy(bf16[1,2048,384]{1,2,0:T(8,128)(2,1)S(1)} %fusion.22) | data formatting | bytes 3145728 | tf_op jit(solution)/shard_map/reshape | solution.py:143
  198.9 34.3 %reduce = bf16[2048,384]{1,0:T(8,128)(2,1)S(1)} reduce(bf16[2048,1,384]{2,1,0:T(2,128)(2,1)} %bitcast.68, bf16[]{:T(256)} %broadcast.35), dimensions={1}, to_apply=%bitcast.50.reduce_sub_computation | reduce | bytes 3145730
  233.2 1.9 reshape.111
  235.0 14.1 %convolution_convert_fusion = bf16[8,384,3072]{2,1,0:T(8,128)(2,1)} fusion(bf16[8,256,384]{1,2,0:T(8,128)(2,1)} %all-to-all-done.5, bf16[8,256,3072]{2,1,0:T(8,128)(2,1)} %bitcast.70), kind=kOutput, calls=%fused_computation.5 | convolution fusion | flops 4841275392 | bytes 33030144 | tf_op jit(solution)/shard_map/rlp,rle->rpe/dot_general | solution.py:134
  249.1 12.8 %convert_reduce_fusion = f32[384,3072]{1,0:T(8,128)} fusion(bf16[8,384,3072]{2,1,0:T(8,128)(2,1)} %convolution_convert_fusion), kind=kLoop, calls=%fused_computation.2 | loop fusion | flops 17694720 | bytes 23592960 | tf_op jit(solution)/shard_map/reduce_sum | solution.py:138
  261.9 5.5 %reshape_reshape.9 = f32[16,2,12,3072]{3,2,1,0:T(8,128)} reshape(f32[384,3072]{1,0:T(8,128)} %convert_reduce_fusion) | data formatting | bytes 9437184 | tf_op jit(solution)/shard_map/reshape;reshape | solution.py:33
  267.4 5.5 %copy.137 = f32[2,16,12,3072]{3,1,2,0:T(8,128)S(1)} copy(f32[2,16,12,3072]{3,2,0,1:T(8,128)} %bitcast.66) | data formatting | bytes 9437184 | tf_op jit(solution)/shard_map/transpose | solution.py:33
  272.9 8.6 %all_to_all.50 = f32[2,16,12,3072]{3,1,2,0:T(8,128)} all-to-all(f32[2,16,12,3072]{3,1,2,0:T(8,128)S(1)} %copy.137), channel_id=1, replica_groups=mesh['group_0'=8,'group_1'=2,'group_2'=2,'rep'=8] {'group_2'}, dimensions={0} | all-to-all | bytes 9437184 | tf_op jit(solution)/shard_map/all_to_all | solution.py:38
  281.6 6.9 %all-to-all-start.4 = ((bf16[8,2,49152]{2,1,0:T(2,128)(2,1)}), bf16[8,2,49152]{2,1,0:T(2,128)(2,1)}, u32[]{:S(2)}, u32[]{:S(2)}) async-start(bf16[8,2,49152]{2,1,0:T(2,128)(2,1)} %reshape.111), calls=%async_computation.4 | async-start | bytes 3145728 | tf_op jit(solution)/shard_map/all_to_all | solution.py:142
  288.5 2.9 reduce_sum.50
  291.4 3.0 copy.138
  294.4 14.6 %all-to-all-done.4 = bf16[8,2,49152]{2,1,0:T(2,128)(2,1)} async-done(((bf16[8,2,49152]{2,1,0:T(2,128)(2,1)}), bf16[8,2,49152]{2,1,0:T(2,128)(2,1)}, u32[]{:S(2)}, u32[]{:S(2)}) %all-to-all-start.4) | async-done | bytes 1572896 | tf_op jit(solution)/shard_map/all_to_all | solution.py:142
  309.0 6.4 %all-to-all-start.7 = ((f32[16,12,3072]{2,1,0:T(8,128)}), f32[16,12,3072]{2,1,0:T(8,128)}, u32[]{:S(2)}, u32[]{:S(2)}) async-start(f32[16,12,3072]{2,1,0:T(8,128)} %copy.138), calls=%async_computation.7 | async-start | bytes 6291456 | tf_op jit(solution)/shard_map/all_to_all | solution.py:46
  315.5 6.3 %reshape.112 = bf16[2048,1,384]{2,1,0:T(2,128)(2,1)} reshape(bf16[8,2,49152]{2,1,0:T(2,128)(2,1)} %all-to-all-done.4) | data formatting | bytes 3145728
  321.8 6.8 %copy.124 = bf16[1,2048,384]{1,2,0:T(8,128)(2,1)S(1)} copy(bf16[1,2048,384]{2,0,1:T(2,128)(2,1)} %bitcast.69) | data formatting | bytes 3145728 | tf_op jit(solution)/shard_map/all_to_all | solution.py:142
  329.6 1.3 reshape.101
  331.0 5.6 %convolution_convert_fusion.2 = bf16[24,128,256]{2,1,0:T(8,128)(2,1)} fusion(bf16[256,24,128]{0,2,1:T(8,128)(2,1)} %reshape.101, f32[24,256,256]{1,2,0:T(8,128)} %get-tuple-element.74, f32[24,256]{1,0:T(8,128)S(1)} %get-tuple-element.73), kind=kOutput, calls=%fused_computation.25 | convolution fusion | flops 406585344 | bytes 9461760 | tf_op jit(solution)/shard_map/while/body/eval_jaxpr/hqk,qhd->khd/dot_general | solution.py:88
  336.6 2.7 copy.141
  339.3 5.1 %fusion.44 = f32[24,256,256]{1,2,0:T(8,128)} fusion(bf16[256,24,128]{0,2,1:T(8,128)(2,1)} %bitcast.73, bf16[256,24,128]{0,2,1:T(8,128)(2,1)S(1)} %copy-done.2), kind=kOutput, calls=%fused_computation.40 | convolution fusion | flops 402653184 | bytes 9437184 | tf_op jit(solution)/shard_map/while/body/eval_jaxpr/qhd,khd->hqk/dot_general | solution.py:91
  344.3 12.2 %fusion.25 = bf16[24,256,128]{1,2,0:T(8,128)(2,1)} fusion(bf16[256,24,128]{0,2,1:T(8,128)(2,1)} %bitcast.80, f32[24,256,256]{1,2,0:T(8,128)} %fusion.44, f32[24,256,256]{1,2,0:T(8,128)} %get-tuple-element.74, f32[24,256]{1,0:T(8,128)S(1)} %get-tuple-element.73), kind=kOutput, calls=%fused_computation.22 | convolution fusion | flops 414456064 | bytes 15753216 | tf_op jit(solution)/shard_map/while/body/eval_jaxpr/hqk,khd->qhd/dot_general | solution.py:94
  356.5 2.7 copy.139
  359.2 11.9 %fusion.28 = bf16[24,256,128]{1,2,0:T(8,128)(2,1)} fusion(bf16[256,24,128]{0,2,1:T(8,128)(2,1)S(1)} %bitcast.78, f32[24,256,256]{1,2,0:T(8,128)} %fusion.44, f32[24,256,256]{1,2,0:T(8,128)} %get-tuple-element.74, f32[24,256]{1,0:T(8,128)S(1)} %get-tuple-element.73), kind=kOutput, calls=%fused_computation.23 | convolution fusion | flops 414456064 | bytes 15753216 | tf_op jit(solution)/shard_map/while/body/eval_jaxpr/hqk,qhd->khd/dot_general | solution.py:95
  371.1 2.6 copy.140
  373.8 15.1 %all-to-all-done.7 = f32[16,12,3072]{2,1,0:T(8,128)} async-done(((f32[16,12,3072]{2,1,0:T(8,128)}), f32[16,12,3072]{2,1,0:T(8,128)}, u32[]{:S(2)}, u32[]{:S(2)}) %all-to-all-start.7) | async-done | bytes 2359328 | tf_op jit(solution)/shard_map/all_to_all | solution.py:46
  388.8 2.8 reduce_sum.51
  (30 shorter events, 5.4 us)
Async XLA Ops:
  7.2 11.5 %copy-start = (bf16[96,3072]{1,0:T(8,128)(2,1)S(1)}, bf16[96,3072]{1,0:T(8,128)(2,1)}, u32[]{:S(2)}) copy-start(bf16[96,3072]{1,0:T(8,128)(2,1)} %param.10) | copy-start | bytes 1769476
  7.2 174.7 %all-gather.3.cloned.1.call-start = ((), (), s32[]{:S(2)}) async-start(), calls=%async_computation.8 | async-start | bytes 14155776 | tf_op jit(solution)/shard_map/all_gather | solution.py:116
  7.9 29.5 %copy-start.4 = (bf16[1,256,3072]{2,1,0:T(8,128)(2,1)S(1)}, bf16[1,256,3072]{2,1,0:T(8,128)(2,1)}, u32[]{:S(2)}) copy-start(bf16[1,256,3072]{2,1,0:T(8,128)(2,1)} %param.6) | copy-start | bytes 4718596
  9.5 18.3 %all-to-all-start.2 = ((bf16[16,12,12]{1,2,0:T(8,128)(2,1)}), bf16[16,12,12]{1,2,0:T(8,128)(2,1)S(1)}, u32[]{:S(2)}, u32[]{:S(2)}) async-start(bf16[16,12,12]{1,2,0:T(8,128)(2,1)} %broadcast_in_dim.52), calls=%async_computation.2 | async-start | bytes 131072 | tf_op jit(solution)/shard_map/all_to_all | solution.py:14
  33.0 44.4 %all-to-all-start = ((bf16[16,12,3072]{2,1,0:T(8,128)(2,1)}), bf16[16,12,3072]{2,1,0:T(8,128)(2,1)}, u32[]{:S(2)}, u32[]{:S(2)}) async-start(bf16[16,12,3072]{2,1,0:T(8,128)(2,1)} %broadcast_in_dim.50), calls=%async_computation | async-start | bytes 3145728 | tf_op jit(solution)/shard_map/all_to_all | solution.py:14
  43.3 7.4 %copy-start.3 = (bf16[1,256,3072]{1,2,0:T(8,128)(2,1)}, bf16[1,256,3072]{1,2,0:T(8,128)(2,1)S(1)}, u32[]{:S(2)}) copy-start(bf16[1,256,3072]{1,2,0:T(8,128)(2,1)S(1)} %copy.149) | copy-start | bytes 4718596
  85.3 149.7 %all-to-all-start.5 = ((bf16[8,256,384]{1,2,0:T(8,128)(2,1)}), bf16[8,256,384]{1,2,0:T(8,128)(2,1)}, u32[]{:S(2)}, u32[]{:S(2)}) async-start(bf16[8,256,384]{1,2,0:T(8,128)(2,1)} %copy.136), calls=%async_computation.5 | async-start | bytes 3145728 | tf_op jit(solution)/shard_map/all_to_all | solution.py:121
  281.6 27.5 %all-to-all-start.4 = ((bf16[8,2,49152]{2,1,0:T(2,128)(2,1)}), bf16[8,2,49152]{2,1,0:T(2,128)(2,1)}, u32[]{:S(2)}, u32[]{:S(2)}) async-start(bf16[8,2,49152]{2,1,0:T(2,128)(2,1)} %reshape.111), calls=%async_computation.4 | async-start | bytes 3145728 | tf_op jit(solution)/shard_map/all_to_all | solution.py:142
  309.0 79.8 %all-to-all-start.7 = ((f32[16,12,3072]{2,1,0:T(8,128)}), f32[16,12,3072]{2,1,0:T(8,128)}, u32[]{:S(2)}, u32[]{:S(2)}) async-start(f32[16,12,3072]{2,1,0:T(8,128)} %copy.138), calls=%async_computation.7 | async-start | bytes 6291456 | tf_op jit(solution)/shard_map/all_to_all | solution.py:46
  336.6 2.7 copy-start.2
  356.5 2.7 copy-start.5
  371.1 20.5 %copy-start.1 = (bf16[96,3072]{1,0:T(8,128)(2,1)S(1)}, bf16[96,3072]{1,0:T(8,128)(2,1)}, u32[]{:S(2)}) copy-start(bf16[96,3072]{1,0:T(8,128)(2,1)} %param.10) | copy-start | bytes 1769476
Sparse Core Ops, SparseCore 0:
  10.6 171.2 all-gather.2
where the time goes:
time: 406 us; the launch traced here: 399 us
  waiting for transfers between devices  125 us (31%)
  local copies, waits for them, and re-layouts  81.5 us (20%)
  matrix products  71.7 us (18%)
  other arithmetic  53.3 us (13%)
  starting transfers between devices  35 us (9%)
  blocking collectives  18 us (4%)
  between operations  14.5 us (4%)
    all_gather x1, waiting for transfers between devices, per_device(): all_output = lax.all_gather(output_flat, 'rep', axis=0, tiled=True)  77.1 us
    unnamed x1, other arithmetic  34.3 us
    unnamed x22, local copies, waits for them, and re-layouts  17.7 us
    all_to_all x2, waiting for transfers between devices, from_everyone(): lax.all_to_all(jnp.broadcast_to(value[None], (count, *value.shape)), axis...  17.3 us
    all_to_all x1, waiting for transfers between devices, sum_in_two_steps(): lax.all_to_all(nearer, far, split_axis=0, concat_axis=0, tiled=True)  15.1 us
    all_to_all x1, waiting for transfers between devices, per_device(): lax.all_to_all(grad_columns.reshape(1, replica_count * local_rows, group_...  14.6 us
    dot_general x1, matrix products, per_device(): jnp.einsum('rlp,rle->rpe', gathered_ctx, output_blocks, preferred_element...  14.1 us
    all_to_all x2, starting transfers between devices, from_everyone(): lax.all_to_all(jnp.broadcast_to(value[None], (count, *value.shape)), axis...  13.6 us
  transfers between devices with their start and end apart: 6, of which 5 were waited for; matrix products, arithmetic and copies ran while one was open for 42% of the time, Pallas kernels for 0%

commit v1 on v0

--- a/solution.py
+++ b/solution.py
@@ -3,6 +3,7 @@
 from jax import lax
 from jax.sharding import Mesh
 from jax.sharding import PartitionSpec as P
+from jax.lax import all_to_all, axis_size
 
 HD = 128
 GROUP = ("group_0", "group_1", "group_2")
@@ -113,7 +114,9 @@
     first_row = lax.axis_index("rep") * slab_rows
     codes_part = lax.dynamic_slice_in_dim(weight_codes, first_row, slab_rows, 0)
     scales_part = lax.dynamic_slice_in_dim(weight_scales, first_row, slab_rows, 0)
-    all_output = lax.all_gather(output_flat, "rep", axis=0, tiled=True)
+    all_output = jnp.concatenate(
+        all_to_all(jnp.stack(axis_size("rep") * [output_flat], 0), "rep", 0, 0), 0
+    )
     split_context = jnp.moveaxis(
         context_flat.reshape(local_rows, group_count, replica_count, slab_rows), 2, 0
     )

time: 406 us -> 461 us (1.14)
  waiting for transfers between devices: 125 us -> 174 us
  local copies, waits for them, and re-layouts: 81.5 us -> 96.3 us
  between operations: 14.5 us -> 1.05 us
  starting transfers between devices: 35 us -> 42 us
  other arithmetic: 53.3 us -> 59 us
    all_to_all x0 -> x1, waiting for transfers between devices: none -> 96.7 us  [per_device(): all_to_all(jnp.stack(axis_size('rep') * [output_flat], 0), 'rep', 0, 0)]
    all_gather x1 -> x0, waiting for transfers between devices: 77.1 us -> none  [per_device(): all_output = lax.all_gather(output_flat, 'rep', axis=0, tiled=True)]
    all_to_all x2 -> x3, waiting for transfers between devices: 17.3 us -> 47.4 us  [from_everyone(): lax.all_to_all(jnp.broadcast_to(value[None], (count, *value.shape)), axis...]
    mul x2 -> x0, local copies, waits for them, and re-layouts: 8.51 us -> none  [restore(): code_rows.astype(jnp.float32).reshape(row_count, block_count, -1)]
    all_to_all x0 -> x1, starting transfers between devices: none -> 7.78 us  [per_device(): all_to_all(jnp.stack(axis_size('rep') * [output_flat], 0), 'rep', 0, 0)]
    another operation x0 -> x1, local copies, waits for them, and re-layouts: none -> 7.58 us  [per_device(): jnp.stack(axis_size('rep') * [output_flat], 0)]
    convert_element_type x0 -> x1, local copies, waits for them, and re-layouts: none -> 4.84 us  [restore(): return spread.reshape(row_count, -1).astype(jnp.bfloat16)]
    all_to_all x2 -> x1, blocking collectives: 9.34 us -> 5.63 us  [from_everyone(): lax.all_to_all(jnp.broadcast_to(value[None], (count, *value.shape)), axis...]
  transfers between devices with their start and end apart: 6 -> 7, of which waited for: 5 -> 6; matrix products, arithmetic and copies ran while one was open for 42% -> 38% of each run, Pallas kernels for 0% -> 0%
where the time goes in v1:
time: 461 us; the launch traced here: 456 us
  waiting for transfers between devices  174 us (38%)
  local copies, waits for them, and re-layouts  96.3 us (21%)
  matrix products  69.7 us (15%)
  other arithmetic  59 us (13%)
  starting transfers between devices  42 us (9%)
  blocking collectives  14.2 us (3%)
    all_to_all x1, waiting for transfers between devices, per_device(): all_to_all(jnp.stack(axis_size('rep') * [output_flat], 0), 'rep', 0, 0)  96.7 us
    all_to_all x3, waiting for transfers between devices, from_everyone(): lax.all_to_all(jnp.broadcast_to(value[None], (count, *value.shape)), axis...  47.4 us
    unnamed x1, other arithmetic  35.5 us
    unnamed x20, local copies, waits for them, and re-layouts  20.1 us
    all_to_all x3, starting transfers between devices, from_everyone(): lax.all_to_all(jnp.broadcast_to(value[None], (count, *value.shape)), axis...  16.1 us
    all_to_all x1, waiting for transfers between devices, sum_in_two_steps(): lax.all_to_all(nearer, far, split_axis=0, concat_axis=0, tiled=True)  15.7 us
    all_to_all x1, waiting for transfers between devices, per_device(): lax.all_to_all(grad_columns.reshape(1, replica_count * local_rows, group_...  14.3 us
    dot_general x1, matrix products, per_device(): jnp.einsum('rlp,rle->rpe', gathered_ctx, output_blocks, preferred_element...  13.8 us
  transfers between devices with their start and end apart: 7, of which 6 were waited for; matrix products, arithmetic and copies ran while one was open for 38% of the time, Pallas kernels for 0%

profile of v1, /device:TPU:4, one launch (start us, length us, event | category | flops | bytes accessed | tf_op | source)
XLA Modules:
  0.0 456.4 jit_solution(2358437438961326919)
XLA Ops:
  2.1 9.2 %all-to-all-start.2 = ((bf16[16,12,12]{1,2,0:T(8,128)(2,1)}), bf16[16,12,12]{1,2,0:T(8,128)(2,1)S(1)}, u32[]{:S(2)}, u32[]{:S(2)}) async-start(bf16[16,12,12]{1,2,0:T(8,128)(2,1)} %broadcast_in_dim.52), calls=%async_computation.2 | async-start | bytes 131072 | tf_op jit(solution)/shard_map/all_to_all | solution.py:15
  11.4 9.0 %all-to-all-done.2 = bf16[16,12,12]{1,2,0:T(8,128)(2,1)S(1)} async-done(((bf16[16,12,12]{1,2,0:T(8,128)(2,1)}), bf16[16,12,12]{1,2,0:T(8,128)(2,1)S(1)}, u32[]{:S(2)}, u32[]{:S(2)}) %all-to-all-start.2) | async-done | bytes 4640 | tf_op jit(solution)/shard_map/all_to_all | solution.py:15
  21.7 3.7 all-to-all-start
  26.2 37.7 %all-to-all-done = bf16[16,12,3072]{2,1,0:T(8,128)(2,1)S(1)} async-done(((bf16[16,12,3072]{2,1,0:T(8,128)(2,1)}), bf16[16,12,3072]{2,1,0:T(8,128)(2,1)S(1)}, u32[]{:S(2)}, u32[]{:S(2)}) %all-to-all-start) | async-done | bytes 1179680 | tf_op jit(solution)/shard_map/all_to_all | solution.py:15
  63.9 3.2 all-to-all-start.3
  68.8 5.6 %all_to_all.53 = bf16[2,16,12,3072]{3,1,2,0:T(8,128)(2,1)S(1)} all-to-all(bf16[2,16,12,3072]{3,1,2,0:T(8,128)(2,1)S(1)} %broadcast_in_dim.51), channel_id=1, replica_groups=mesh['group_0'=8,'group_1'=2,'group_2'=2,'rep'=8] {'group_2'}, dimensions={0} | all-to-all | bytes 4718592 | tf_op jit(solution)/shard_map/all_to_all | solution.py:15
  74.4 7.6 %stack.3 = bf16[8,256,3072]{2,1,0:T(8,128)(2,1)} broadcast(bf16[256,3072]{1,0:T(8,128)(2,1)} %bitcast.70), dimensions={1,2} | broadcast | bytes 14155776 | tf_op jit(solution)/shard_map/stack | solution.py:118
  82.0 7.8 %all-to-all-start.4 = ((bf16[8,256,3072]{2,1,0:T(8,128)(2,1)}), bf16[8,256,3072]{2,1,0:T(8,128)(2,1)}, u32[]{:S(2)}, u32[]{:S(2)}) async-start(bf16[8,256,3072]{2,1,0:T(8,128)(2,1)} %stack.3), calls=%async_computation.4 | async-start | bytes 25165824 | tf_op jit(solution)/shard_map/all_to_all | solution.py:118
  89.8 2.6 copy.156
  92.4 2.6 copy.154
  94.9 2.6 copy.155
  97.5 6.8 %fusion.36 = (f32[24,256]{1,0:T(8,128)S(1)}, f32[24,256,256]{1,2,0:T(8,128)}) fusion(bf16[256,24,128]{0,2,1:T(8,128)(2,1)} %bitcast.73, bf16[256,24,128]{0,2,1:T(8,128)(2,1)} %bitcast.71), kind=kOutput, calls=%fused_computation.36 | convolution fusion | flops 407372032 | bytes 9461760 | tf_op jit(solution)/shard_map/while/body/eval_jaxpr/sub | solution.py:71
  104.3 5.1 %fusion.26 = bf16[256,24,128]{0,2,1:T(8,128)(2,1)} fusion(bf16[256,24,128]{0,2,1:T(8,128)(2,1)} %bitcast.64, f32[24,256,256]{1,2,0:T(8,128)} %get-tuple-element.74, f32[24,256]{1,0:T(8,128)S(1)} %get-tuple-element.73), kind=kOutput, calls=%fused_computation.26 | convolution fusion | flops 406585344 | bytes 9461760 | tf_op jit(solution)/shard_map/while/body/eval_jaxpr/hqk,khd->qhd/dot_general | solution.py:74
  109.4 3.7 reshape_reshape.8
  113.1 2.3 copy.140
  115.4 1.5 copy.141
  118.0 5.5 %copy.123 = f32[16,2,12,3072]{3,2,1,0:T(8,128)} copy(f32[16,2,12,3072]{3,0,2,1:T(8,128)S(1)} %convert_bitcast_fusion) | data formatting | bytes 9437184 | tf_op jit(solution)/shard_map/convert_element_type | solution.py:55
  123.5 7.8 %reshape.116 = f32[384,12,256]{2,1,0:T(8,128)} reshape(f32[16,2,12,3072]{3,2,1,0:T(8,128)} %copy.123) | data formatting | bytes 9437184 | tf_op jit(solution)/shard_map/convert_element_type | solution.py:55
  131.3 96.7 %all-to-all-done.4 = bf16[8,256,3072]{2,1,0:T(8,128)(2,1)} async-done(((bf16[8,256,3072]{2,1,0:T(8,128)(2,1)}), bf16[8,256,3072]{2,1,0:T(8,128)(2,1)}, u32[]{:S(2)}, u32[]{:S(2)}) %all-to-all-start.4) | async-done | bytes 12582944 | tf_op jit(solution)/shard_map/all_to_all | solution.py:118
  228.0 6.2 %all-to-all-start.6 = ((bf16[8,256,384]{1,2,0:T(8,128)(2,1)}), bf16[8,256,384]{1,2,0:T(8,128)(2,1)S(1)}, u32[]{:S(2)}, u32[]{:S(2)}) async-start(bf16[8,256,384]{1,2,0:T(8,128)(2,1)} %copy.141), calls=%async_computation.6 | async-start | bytes 3145728 | tf_op jit(solution)/shard_map/all_to_all | solution.py:124
  234.2 4.5 multiply_convert_fusion.1
  238.7 4.8 %copy.127 = bf16[384,12,256]{0,2,1:T(8,128)(2,1)} copy(bf16[384,12,256]{2,1,0:T(8,128)(2,1)} %multiply_convert_fusion.1) | data formatting | bytes 4718592 | tf_op jit(solution)/shard_map/convert_element_type | solution.py:57
  243.5 9.7 %fusion.17 = bf16[1,2048,384]{1,2,0:T(8,128)(2,1)} fusion(bf16[384,3072]{0,1:T(8,128)(2,1)} %bitcast.69, bf16[2048,3072]{1,0:T(8,128)(2,1)} %bitcast.4), kind=kOutput, calls=%fused_computation.19 | convolution fusion | flops 4832624640 | bytes 16515072 | tf_op jit(solution)/shard_map/dot_general | solution.py:126
  253.2 8.4 %copy.128 = bf16[1,2048,384]{2,0,1:T(2,128)(2,1)} copy(bf16[1,2048,384]{1,2,0:T(8,128)(2,1)} %fusion.17) | data formatting | bytes 3145728 | tf_op jit(solution)/shard_map/reshape | solution.py:146
  262.2 35.5 %reduce = bf16[2048,384]{1,0:T(8,128)(2,1)} reduce(bf16[2048,1,384]{2,1,0:T(2,128)(2,1)} %bitcast.61, bf16[]{:T(256)} %broadcast.39), dimensions={1}, to_apply=%bitcast.42.reduce_sub_computation | reduce | bytes 3145730
  297.6 3.7 reshape.121
  301.4 13.8 %convolution_convert_fusion = bf16[8,384,3072]{2,1,0:T(8,128)(2,1)} fusion(bf16[8,256,384]{1,2,0:T(8,128)(2,1)S(1)} %all-to-all-done.6, bf16[8,256,3072]{2,1,0:T(8,128)(2,1)} %all-to-all-done.4), kind=kOutput, calls=%fused_computation.3 | convolution fusion | flops 4841275392 | bytes 33030144 | tf_op jit(solution)/shard_map/rlp,rle->rpe/dot_general | solution.py:137
  315.2 12.8 %convert_reduce_fusion = f32[384,3072]{1,0:T(8,128)} fusion(bf16[8,384,3072]{2,1,0:T(8,128)(2,1)} %convolution_convert_fusion), kind=kLoop, calls=%fused_computation.2 | loop fusion | flops 17694720 | bytes 23592960 | tf_op jit(solution)/shard_map/reduce_sum | solution.py:141
  328.0 5.5 %reshape_reshape.9 = f32[16,2,12,3072]{3,2,1,0:T(8,128)} reshape(f32[384,3072]{1,0:T(8,128)} %convert_reduce_fusion) | data formatting | bytes 9437184 | tf_op jit(solution)/shard_map/reshape;reshape | solution.py:34
  333.5 5.5 %copy.142 = f32[2,16,12,3072]{3,1,2,0:T(8,128)S(1)} copy(f32[2,16,12,3072]{3,2,0,1:T(8,128)} %bitcast.60) | data formatting | bytes 9437184 | tf_op jit(solution)/shard_map/transpose | solution.py:34
  339.0 8.6 %all_to_all.54 = f32[2,16,12,3072]{3,1,2,0:T(8,128)} all-to-all(f32[2,16,12,3072]{3,1,2,0:T(8,128)S(1)} %copy.142), channel_id=1, replica_groups=mesh['group_0'=8,'group_1'=2,'group_2'=2,'rep'=8] {'group_2'}, dimensions={0} | all-to-all | bytes 9437184 | tf_op jit(solution)/shard_map/all_to_all | solution.py:39
  347.6 7.2 %all-to-all-start.5 = ((bf16[8,2,49152]{2,1,0:T(2,128)(2,1)}), bf16[8,2,49152]{2,1,0:T(2,128)(2,1)}, u32[]{:S(2)}, u32[]{:S(2)}) async-start(bf16[8,2,49152]{2,1,0:T(2,128)(2,1)} %reshape.121), calls=%async_computation.5 | async-start | bytes 3145728 | tf_op jit(solution)/shard_map/all_to_all | solution.py:145
  354.8 2.9 reduce_sum.50
  357.8 3.1 copy.143
  360.8 14.3 %all-to-all-done.5 = bf16[8,2,49152]{2,1,0:T(2,128)(2,1)} async-done(((bf16[8,2,49152]{2,1,0:T(2,128)(2,1)}), bf16[8,2,49152]{2,1,0:T(2,128)(2,1)}, u32[]{:S(2)}, u32[]{:S(2)}) %all-to-all-start.5) | async-done | bytes 1572896 | tf_op jit(solution)/shard_map/all_to_all | solution.py:145
  375.1 4.7 %all-to-all-start.8 = ((f32[16,12,3072]{2,1,0:T(8,128)}), f32[16,12,3072]{2,1,0:T(8,128)}, u32[]{:S(2)}, u32[]{:S(2)}) async-start(f32[16,12,3072]{2,1,0:T(8,128)} %copy.143), calls=%async_computation.8 | async-start | bytes 6291456 | tf_op jit(solution)/shard_map/all_to_all | solution.py:47
  379.8 6.3 %reshape.122 = bf16[2048,1,384]{2,1,0:T(2,128)(2,1)} reshape(bf16[8,2,49152]{2,1,0:T(2,128)(2,1)} %all-to-all-done.5) | data formatting | bytes 3145728
  386.2 6.8 %copy.129 = bf16[1,2048,384]{1,2,0:T(8,128)(2,1)S(1)} copy(bf16[1,2048,384]{2,0,1:T(2,128)(2,1)} %bitcast.62) | data formatting | bytes 3145728 | tf_op jit(solution)/shard_map/all_to_all | solution.py:145
  393.9 1.3 reshape.113
  395.3 5.7 %fusion.37 = f32[24,256,256]{1,2,0:T(8,128)} fusion(bf16[256,24,128]{0,2,1:T(8,128)(2,1)} %bitcast.65, bf16[256,24,128]{0,2,1:T(8,128)(2,1)} %reshape.113), kind=kOutput, calls=%fused_computation.38 | convolution fusion | flops 402653184 | bytes 9437184 | tf_op jit(solution)/shard_map/while/body/eval_jaxpr/qhd,khd->hqk/dot_general | solution.py:92
  401.0 11.8 %fusion.21 = bf16[24,256,128]{1,2,0:T(8,128)(2,1)} fusion(bf16[256,24,128]{0,2,1:T(8,128)(2,1)S(1)} %bitcast.74, f32[24,256,256]{1,2,0:T(8,128)} %fusion.37, f32[24,256,256]{1,2,0:T(8,128)} %get-tuple-element.74, f32[24,256]{1,0:T(8,128)S(1)} %get-tuple-element.73), kind=kOutput, calls=%fused_computation.21 | convolution fusion | flops 414456064 | bytes 15753216 | tf_op jit(solution)/shard_map/while/body/eval_jaxpr/hqk,qhd->khd/dot_general | solution.py:96
  412.8 2.7 copy.145
  415.5 11.7 %fusion.18 = bf16[24,256,128]{1,2,0:T(8,128)(2,1)} fusion(bf16[256,24,128]{0,2,1:T(8,128)(2,1)S(1)} %bitcast.72, f32[24,256,256]{1,2,0:T(8,128)} %fusion.37, f32[24,256,256]{1,2,0:T(8,128)} %get-tuple-element.74, f32[24,256]{1,0:T(8,128)S(1)} %get-tuple-element.73), kind=kOutput, calls=%fused_computation.20 | convolution fusion | flops 414456064 | bytes 15753216 | tf_op jit(solution)/shard_map/while/body/eval_jaxpr/hqk,khd->qhd/dot_general | solution.py:95
  427.2 2.7 copy.144
  429.9 5.1 %convolution_convert_fusion.3 = bf16[24,128,256]{2,1,0:T(8,128)(2,1)} fusion(bf16[256,24,128]{0,2,1:T(8,128)(2,1)S(1)} %copy-done.2, f32[24,256,256]{1,2,0:T(8,128)} %get-tuple-element.74, f32[24,256]{1,0:T(8,128)S(1)} %get-tuple-element.73), kind=kOutput, calls=%fused_computation.23 | convolution fusion | flops 406585344 | bytes 9461760 | tf_op jit(solution)/shard_map/while/body/eval_jaxpr/hqk,qhd->khd/dot_general | solution.py:89
  435.0 2.6 copy.146
  437.7 15.7 %all-to-all-done.8 = f32[16,12,3072]{2,1,0:T(8,128)} async-done(((f32[16,12,3072]{2,1,0:T(8,128)}), f32[16,12,3072]{2,1,0:T(8,128)}, u32[]{:S(2)}, u32[]{:S(2)}) %all-to-all-start.8) | async-done | bytes 2359328 | tf_op jit(solution)/shard_map/all_to_all | solution.py:47
  453.4 2.8 reduce_sum.51
  (29 shorter events, 7.9 us)
Async XLA Ops:
  0.6 10.7 %copy-start = (bf16[96,3072]{1,0:T(8,128)(2,1)S(1)}, bf16[96,3072]{1,0:T(8,128)(2,1)}, u32[]{:S(2)}) copy-start(bf16[96,3072]{1,0:T(8,128)(2,1)} %param.10) | copy-start | bytes 1769476
  2.1 18.3 %all-to-all-start.2 = ((bf16[16,12,12]{1,2,0:T(8,128)(2,1)}), bf16[16,12,12]{1,2,0:T(8,128)(2,1)S(1)}, u32[]{:S(2)}, u32[]{:S(2)}) async-start(bf16[16,12,12]{1,2,0:T(8,128)(2,1)} %broadcast_in_dim.52), calls=%async_computation.2 | async-start | bytes 131072 | tf_op jit(solution)/shard_map/all_to_all | solution.py:15
  21.7 42.2 %all-to-all-start = ((bf16[16,12,3072]{2,1,0:T(8,128)(2,1)}), bf16[16,12,3072]{2,1,0:T(8,128)(2,1)S(1)}, u32[]{:S(2)}, u32[]{:S(2)}) async-start(bf16[16,12,3072]{2,1,0:T(8,128)(2,1)} %broadcast_in_dim.50), calls=%async_computation | async-start | bytes 3145728 | tf_op jit(solution)/shard_map/all_to_all | solution.py:15
  63.9 4.6 %all-to-all-start.3 = ((bf16[2,2,1152]{2,1,0:T(2,128)(2,1)}), bf16[2,2,1152]{2,1,0:T(2,128)(2,1)S(1)}, u32[]{:S(2)}, u32[]{:S(2)}) async-start(bf16[2,2,1152]{2,1,0:T(2,128)(2,1)} %reshape.119), calls=%async_computation.3 | async-start | bytes 18432 | tf_op jit(solution)/shard_map/all_to_all | solution.py:15
  82.0 146.0 %all-to-all-start.4 = ((bf16[8,256,3072]{2,1,0:T(8,128)(2,1)}), bf16[8,256,3072]{2,1,0:T(8,128)(2,1)}, u32[]{:S(2)}, u32[]{:S(2)}) async-start(bf16[8,256,3072]{2,1,0:T(8,128)(2,1)} %stack.3), calls=%async_computation.4 | async-start | bytes 25165824 | tf_op jit(solution)/shard_map/all_to_all | solution.py:118
  228.0 73.4 %all-to-all-start.6 = ((bf16[8,256,384]{1,2,0:T(8,128)(2,1)}), bf16[8,256,384]{1,2,0:T(8,128)(2,1)S(1)}, u32[]{:S(2)}, u32[]{:S(2)}) async-start(bf16[8,256,384]{1,2,0:T(8,128)(2,1)} %copy.141), calls=%async_computation.6 | async-start | bytes 3145728 | tf_op jit(solution)/shard_map/all_to_all | solution.py:124
  347.6 27.5 %all-to-all-start.5 = ((bf16[8,2,49152]{2,1,0:T(2,128)(2,1)}), bf16[8,2,49152]{2,1,0:T(2,128)(2,1)}, u32[]{:S(2)}, u32[]{:S(2)}) async-start(bf16[8,2,49152]{2,1,0:T(2,128)(2,1)} %reshape.121), calls=%async_computation.5 | async-start | bytes 3145728 | tf_op jit(solution)/shard_map/all_to_all | solution.py:145
  375.1 78.3 %all-to-all-start.8 = ((f32[16,12,3072]{2,1,0:T(8,128)}), f32[16,12,3072]{2,1,0:T(8,128)}, u32[]{:S(2)}, u32[]{:S(2)}) async-start(f32[16,12,3072]{2,1,0:T(8,128)} %copy.143), calls=%async_computation.8 | async-start | bytes 6291456 | tf_op jit(solution)/shard_map/all_to_all | solution.py:47
  395.3 5.7 %copy-start.4 = (bf16[1,256,3072]{1,2,0:T(8,128)(2,1)S(1)}, bf16[1,256,3072]{1,2,0:T(8,128)(2,1)}, u32[]{:S(2)}) copy-start(bf16[1,256,3072]{1,2,0:T(8,128)(2,1)} %copy.155) | copy-start | bytes 4718596
  412.8 2.7 copy-start.3
  427.2 2.7 copy-start.2
  435.0 21.1 %copy-start.1 = (bf16[96,3072]{1,0:T(8,128)(2,1)S(1)}, bf16[96,3072]{1,0:T(8,128)(2,1)}, u32[]{:S(2)}) copy-start(bf16[96,3072]{1,0:T(8,128)(2,1)} %param.10) | copy-start | bytes 1769476
